TPU v7x, 512 devices: a whole 4x8x8 slice. The times are simulated.
512 devices in a mesh: seq: 64 (over x, z, core), head: 8 (over y).
Axes of the slice: x: 4, y: 8, z: 8, core: 2. Of those that a mesh axis runs over, the one named last changes fastest.
Arguments:
- queries: bfloat16 [16384, 4096], P('seq', 'head'), may hold values from -6 to 6
- keys: bfloat16 [16384, 4096], P('seq', 'head'), may hold values from -6 to 6
- values: bfloat16 [16384, 4096], P('seq', 'head'), may hold values from -6 to 6
- gate: bfloat16 [16384, 4096], P('seq', 'head'), may hold values from -6 to 6
- residual: bfloat16 [16384, 4096], P('seq', 'head'), may hold values from -40 to 40
- log_decay: float32 [16384, 32], P('seq', 'head'), may hold values from -1 to 0, as said below
- out_weight: bfloat16 [4096, 4096], P('seq', 'head'), may hold values from -0.09375 to 0.09375
- norm_gain: bfloat16 [4096], P('head'), may hold values from 0.099609375 to 1.8984375
- kv_weight: bfloat16 [4096, 2048], P('seq', 'head'), may hold values from -0.09375 to 0.09375
Outputs:
- cache_keys: bfloat16 [16384, 1024], P('seq', 'head')
- cache_values: bfloat16 [16384, 1024], P('seq', 'head')
Inputs may be any that keep to these rules, and one draw needn't show every extreme that they name: `log_decay`: every entry is negative.
All inputs are finite; a program needn't handle non-finite values.
Results may differ from a plain program's by a relative error of at most 0.015.
Values may be sent and summed in bfloat16 or wider, within the bound.
A program may use at most 64 MiB of HBM per device.

v0:
```python
import jax
import jax.numpy as jnp
from jax import lax
from jax.sharding import PartitionSpec as P

HIGHEST = lax.Precision.HIGHEST


def entering(part, axis, combine, identity):
    place = lax.axis_index(axis)
    gathered = jax.tree.map(lambda a: lax.all_gather(a, axis), part)
    state = jax.tree.map(lambda a, e: jnp.zeros_like(a) + jnp.asarray(e, a.dtype), part, identity)

    def one(step, state):
        return combine(
            state, jax.tree.map(lambda a: lax.dynamic_index_in_dim(a, step, 0, False), gathered)
        )

    return lax.fori_loop(0, place, one, state)


def local_retention(queries, keys, values, log_decay, block):
    tokens, heads, width = queries.shape
    count = tokens // block

    def to_blocks(array):
        return array.reshape((count, block) + array.shape[1:])

    lower = jnp.arange(block)[:, None] >= jnp.arange(block)[None, :]

    def advance(carry, inputs):
        state, offset = carry
        query_block, key_block, value_block, decay_block = inputs
        within = jnp.cumsum(decay_block, axis=0)
        spread = within[:, None, :] - within[None, :, :]
        factor = jnp.where(
            lower[:, :, None], jnp.exp(jnp.where(lower[:, :, None], spread, 0.0)), 0.0
        )
        scores = jnp.einsum(
            "ihd,jhd->hij", query_block, key_block, preferred_element_type=jnp.float32
        )
        weighted = scores * jnp.transpose(factor, (2, 0, 1))
        values_wide = value_block.astype(jnp.float32)
        intra = jnp.einsum("hij,jhd->ihd", weighted, values_wide, precision=HIGHEST)
        query_wide = query_block.astype(jnp.float32)
        carried = jnp.exp(within)[:, :, None] * jnp.einsum(
            "ihd,hde->ihe", query_wide, state, precision=HIGHEST
        )
        ending = within[-1]
        key_wide = key_block.astype(jnp.float32) * jnp.exp(ending[None, :] - within)[:, :, None]
        fresh = jnp.exp(ending)[:, None, None] * state + jnp.einsum(
            "jhd,jhe->hde", key_wide, values_wide, precision=HIGHEST
        )
        return ((fresh, offset + ending), (intra + carried, offset[None, :] + within))

    start = (jnp.zeros((heads, width, width), jnp.float32), jnp.zeros((heads,), jnp.float32))
    final, stacked = lax.scan(
        advance,
        start,
        (to_blocks(queries), to_blocks(keys), to_blocks(values), to_blocks(log_decay)),
    )
    return (
        stacked[0].reshape(tokens, heads, width),
        stacked[1].reshape(tokens, heads),
        final[0],
        final[1],
    )


def combine_states(earlier, later):
    return (earlier[0] * later[0], later[0][:, None, None] * earlier[1] + later[1])


def on_device(queries, keys, values, gate, residual, log_decay, out_weight, norm_gain, kv_weight):
    tokens = queries.shape[0]
    heads = log_decay.shape[1]
    width = queries.shape[1] // heads
    shaped = [array.reshape(tokens, heads, width) for array in (queries, keys, values)]
    partial_out, running, state, offset = local_retention(
        shaped[0], shaped[1], shaped[2], log_decay, min(512, tokens)
    )
    identity = (jnp.ones((heads,), jnp.float32), jnp.zeros((heads, width, width), jnp.float32))
    scan_decay, incoming = entering((jnp.exp(offset), state), "seq", combine_states, identity)
    retained = partial_out + jnp.exp(running)[:, :, None] * jnp.einsum(
        "thd,hde->the", shaped[0].astype(jnp.float32), incoming, precision=HIGHEST
    )
    scale = lax.rsqrt(jnp.mean(retained * retained, axis=2, keepdims=True) + 1e-06)
    mixed = (
        jax.nn.silu(gate.astype(jnp.float32)) * (retained * scale).reshape(tokens, heads * width)
    ).astype(jnp.bfloat16)
    all_heads = lax.all_gather(mixed, "head", axis=1, tiled=True)
    out_full, kv_full = (
        lax.all_gather(out_weight, "seq", axis=0, tiled=True),
        lax.all_gather(kv_weight, "seq", axis=0, tiled=True),
    )
    branch = jnp.dot(all_heads, out_full, preferred_element_type=jnp.float32)
    hidden = (residual.astype(jnp.float32) + branch).astype(jnp.bfloat16)
    wide = hidden.astype(jnp.float32)
    squares = lax.psum(jnp.sum(wide * wide, axis=1), "head")
    features = wide.shape[1] * lax.axis_size("head")
    inverse = lax.rsqrt(squares[:, None] / features + 1e-06)
    local_norm = (wide * inverse * norm_gain.astype(jnp.float32)[None, :]).astype(jnp.bfloat16)
    normalized = lax.all_gather(local_norm, "head", axis=1, tiled=True)
    projected = jnp.dot(normalized, kv_full, preferred_element_type=jnp.float32)
    cache_heads = kv_weight.shape[1] // (2 * width)
    arranged = projected.reshape(tokens, cache_heads, 2, width)
    cache_keys = arranged[:, :, 0, :].reshape(tokens, cache_heads * width).astype(jnp.bfloat16)
    cache_values = arranged[:, :, 1, :].reshape(tokens, cache_heads * width).astype(jnp.bfloat16)
    return (cache_keys, cache_values)


def solution(mesh):
    placed = (
        P("seq", "head"),
        P("seq", "head"),
        P("seq", "head"),
        P("seq", "head"),
        P("seq", "head"),
        P("seq", "head"),
        P("seq", "head"),
        P("head"),
        P("seq", "head"),
    )
    return jax.shard_map(
        on_device,
        mesh=mesh,
        in_specs=placed,
        out_specs=(P("seq", "head"), P("seq", "head")),
        check_vma=False,
    )
```

profile of v0, /device:TPU:2, one launch (start us, length us, event | category | flops | bytes accessed | tf_op | source)
XLA Modules:
  0.0 390.9 jit_solution(8764286394529594663)
XLA Ops:
  7.2 0.7 reshape.72
  8.0 1.2 reduce-window.6
  9.2 0.1 slice.23
  9.2 0.1 copy.57
  9.4 0.1 copy.58
  9.5 0.1 add_bitcast_fusion
  9.6 0.2 slice_reduce_fusion
  9.8 0.1 bitcast_exponential_fusion
  9.8 1.1 copy.73
  10.9 2.0 convolution_add_fusion.1
  13.0 0.0 all-gather.10.cloned.1.call-start
  13.1 0.7 all-gather.10.cloned.1.call-update
  13.8 44.7 %all-gather.1 = f32[64,1,4]{2,1,0:T(1,128)S(1)} all-gather(f32[1,1,4]{2,1,0:T(1,128)S(1)} %bitcast.97), channel_id=1, replica_groups=mesh['seq'=64,'head'=8] {'seq'}, dimensions={0}, use_global_device_ids=true | all-gather | bytes 1040 | tf_op jit(solution)/shard_map/all_gather | solution.py:11
  58.6 0.4 fusion.2
  59.0 0.4 convolution_multiply_fusion
  59.4 63.1 %all-gather.16.cloned.1.call-done = f32[256,128,128]{2,1,0:T(8,128)} async-done(((f32[4,128,128]{2,1,0:T(8,128)}), f32[256,128,128]{2,1,0:T(8,128)}) %all-gather.16.cloned.1.call-update) | async-done | bytes 16777232 | tf_op jit(solution)/shard_map/all_gather | solution.py:11
  122.5 17.8 %while.3 = (s32[]{:T(128)}, f32[4,128,128]{2,1,0:T(8,128)S(1)}, s32[]{:T(128)}, f32[64,4]{1,0:T(8,128)S(1)}, f32[64,4,128,128]{3,2,1,0:T(8,128)}, /*index=5*/s32[]{:T(128)}, s32[]{:T(128)}, s32[]{:T(128)}) while((s32[]{:T(128)}, f32[4,128,128]{2,1,0:T(8,128)S(1)}, s32[]{:T(128)}, f32[64,4]{1,0:T(8,128)S(1)}, f32[64,4,128,128]{3,2,1,0:T(8,128)}, ...), condition=%wide.region_3.4_spmd, body=%wide.region_2.3_spmd.sunk | while | flops 131077 | bytes 786607 | solution.py:19
  122.6 1.1 bitcast_add_fusion.2
  123.7 1.1 bitcast_add_fusion.2
  124.8 1.1 bitcast_add_fusion.2
  125.9 1.1 bitcast_add_fusion.2
  127.0 1.1 bitcast_add_fusion.2
  128.1 1.1 bitcast_add_fusion.2
  129.2 1.1 bitcast_add_fusion.2
  130.4 1.1 bitcast_add_fusion.2
  131.5 1.1 bitcast_add_fusion.2
  132.6 1.1 bitcast_add_fusion.2
  133.7 1.1 bitcast_add_fusion.2
  134.8 1.1 bitcast_add_fusion.2
  135.9 1.1 bitcast_add_fusion.2
  137.0 1.1 bitcast_add_fusion.2
  138.1 1.1 bitcast_add_fusion.2
  139.2 1.1 bitcast_add_fusion.2
  140.3 0.4 fusion.3
  140.8 0.8 multiply_reduce_fusion.1
  141.6 0.2 copy.66
  141.8 0.9 fusion.12
  142.8 0.5 all-gather.14.cloned.1.call-update
  143.4 64.4 %all-gather.10.cloned.1.call-done = bf16[4096,512]{1,0:T(8,128)(2,1)} async-done(((bf16[64,512]{1,0:T(8,128)(2,1)}), bf16[4096,512]{1,0:T(8,128)(2,1)}) %all-gather.10.cloned.1.call-update) | async-done | bytes 4194320 | tf_op jit(solution)/shard_map/all_gather | solution.py:93
  207.8 43.4 %all-gather.8.cloned.1.call-done = bf16[256,4096]{1,0:T(8,128)(2,1)} async-done(((bf16[256,512]{1,0:T(8,128)(2,1)}), bf16[256,4096]{1,0:T(8,128)(2,1)}) %all-gather.8.cloned.1.call-update) | async-done | bytes 2097168 | tf_op jit(solution)/shard_map/all_gather | solution.py:91
  251.2 4.2 %multiply_reduce_fusion = (f32[256]{0:T(256)S(1)}, f32[256,512]{1,0:T(8,128)S(1)}) fusion(bf16[256,4096]{1,0:T(8,128)(2,1)} %all-gather.8.cloned.1.call-done, bf16[4096,512]{1,0:T(8,128)(2,1)} %all-gather.10.cloned.1.call-done, bf16[256,512]{1,0:T(8,128)(2,1)S(1)} %copy-done.4), kind=kOutput, calls=%fused_computation.22 | convolution fusion | flops 1074528000 | bytes 7078912 | tf_op jit(solution)/shard_map/dot_general | solution.py:96
  255.3 16.2 %psum.7 = f32[256]{0:T(256)S(1)} all-reduce(f32[256]{0:T(256)S(1)} %get-tuple-element.97), channel_id=1, replica_groups=mesh['seq'=64,'head'=8] {'head'}, use_global_device_ids=true, to_apply=%region_6.7 | all-reduce | flops 256 | bytes 2048 | tf_op jit(solution)/shard_map/psum | solution.py:99
  271.6 0.8 multiply_convert_fusion
  272.4 63.8 %all-gather.14.cloned.1.call-done = bf16[4096,256]{1,0:T(8,128)(2,1)} async-done(((bf16[64,256]{1,0:T(8,128)(2,1)}), bf16[4096,256]{1,0:T(8,128)(2,1)}) %all-gather.14.cloned.1.call-update) | async-done | bytes 2097168 | tf_op jit(solution)/shard_map/all_gather | solution.py:94
  336.2 43.6 %all-gather.12.cloned.1.call-done = bf16[256,4096]{1,0:T(8,128)(2,1)} async-done(((bf16[256,512]{1,0:T(8,128)(2,1)}), bf16[256,4096]{1,0:T(8,128)(2,1)}) %all-gather.12.cloned.1.call-update) | async-done | bytes 2097168 | tf_op jit(solution)/shard_map/all_gather | solution.py:103
  379.8 3.1 convolution_convert_fusion
  382.9 0.7 copy.71
  383.7 0.7 copy.72
  (44 shorter events, 0.6 us)
Async XLA Ops:
  7.2 51.4 %copy-start = (bf16[256,512]{1,0:T(8,128)(2,1)S(1)}, bf16[256,512]{1,0:T(8,128)(2,1)}, u32[]{:S(2)}) copy-start(bf16[256,512]{1,0:T(8,128)(2,1)} %param.11) | copy-start | bytes 786436
  7.2 115.3 %all-gather.16.cloned.1.call-start = ((), (), s32[]{:S(2)}) async-start(), calls=%async_computation.4 | async-start | bytes 17039360 | tf_op jit(solution)/shard_map/all_gather | solution.py:11
  13.0 194.8 %all-gather.10.cloned.1.call-start = ((), (), s32[]{:S(2)}) async-start(), calls=%async_computation.1 | async-start | bytes 4259840 | tf_op jit(solution)/shard_map/all_gather | solution.py:93
  13.8 237.4 %all-gather.8.cloned.1.call-start = ((), (), s32[]{:S(2)}) async-start(), calls=%async_computation | async-start | bytes 2359296 | tf_op jit(solution)/shard_map/all_gather | solution.py:91
  122.5 18.2 %copy-start.1 = (bf16[256,512]{1,0:T(8,128)(2,1)S(1)}, bf16[256,512]{1,0:T(8,128)(2,1)}, u32[]{:S(2)}) copy-start(bf16[256,512]{1,0:T(8,128)(2,1)} %param.13) | copy-start | bytes 786436
  140.8 1.1 copy-start.2
  141.5 1.8 copy-start.3
  141.5 109.7 %copy-start.4 = (bf16[256,512]{1,0:T(8,128)(2,1)S(1)}, bf16[256,512]{1,0:T(8,128)(2,1)}, u32[]{:S(2)}) copy-start(bf16[256,512]{1,0:T(8,128)(2,1)} %param.15) | copy-start | bytes 786436
  142.7 193.4 %all-gather.14.cloned.1.call-start = ((), (), s32[]{:S(2)}) async-start(), calls=%async_computation.3 | async-start | bytes 2129920 | tf_op jit(solution)/shard_map/all_gather | solution.py:94
  143.3 236.5 %all-gather.12.cloned.1.call-start = ((), (), s32[]{:S(2)}) async-start(), calls=%async_computation.2 | async-start | bytes 2359296 | tf_op jit(solution)/shard_map/all_gather | solution.py:103
Sparse Core Ops, SparseCore 0:
  13.1 109.3 all-gather.15
  125.8 81.8 all-gather.9
  209.9 41.2 all-gather.7
  254.4 81.7 all-gather.13
  338.1 41.6 all-gather.11
where the time goes:
time: 393 us; the launch traced here: 391 us
  waiting for transfers between devices  280 us (71%)
  blocking collectives  60.9 us (15%)
  other arithmetic  20.2 us (5%)
  between operations  14 us (4%)
  matrix products  11.3 us (3%)
  local copies, waits for them, and re-layouts  4.19 us (1%)
    all_gather x1, waiting for transfers between devices, on_device(): lax.all_gather(out_weight, 'seq', axis=0, tiled=True)  64.4 us
    all_gather x1, waiting for transfers between devices, on_device(): lax.all_gather(kv_weight, 'seq', axis=0, tiled=True)  63.8 us
    all_gather x1, waiting for transfers between devices, entering(): gathered = jax.tree.map(lambda a: lax.all_gather(a, axis), part)  63.1 us
    all_gather x1, blocking collectives, entering(): gathered = jax.tree.map(lambda a: lax.all_gather(a, axis), part)  44.7 us
    all_gather x1, waiting for transfers between devices, on_device(): normalized = lax.all_gather(local_norm, 'head', axis=1, tiled=True)  43.6 us
    all_gather x1, waiting for transfers between devices, on_device(): all_heads = lax.all_gather(mixed, 'head', axis=1, tiled=True)  43.4 us
    add x16, other arithmetic, combine_states(): later[0][:, None, None] * earlier[1] + later[1]  17 us
    psum x1, blocking collectives, on_device(): squares = lax.psum(jnp.sum(wide * wide, axis=1), 'head')  16.2 us
  transfers between devices with their start and end apart: 5, of which 5 were waited for; matrix products, arithmetic and copies ran while one was open for 6% of the time, Pallas kernels for 0%

commit v1 on v0

--- a/solution.py
+++ b/solution.py
@@ -88,7 +88,12 @@
     mixed = (
         jax.nn.silu(gate.astype(jnp.float32)) * (retained * scale).reshape(tokens, heads * width)
     ).astype(jnp.bfloat16)
-    all_heads = lax.all_gather(mixed, "head", axis=1, tiled=True)
+    ring = [mixed]
+    for hop in range(7):
+        ring.append(lax.ppermute(ring[-1], "head", [(dev, (dev + 1) % 8) for dev in range(8)]))
+    all_heads = jnp.roll(
+        jnp.concatenate(ring[::-1], axis=1), (lax.axis_index("head") + 1) * ring[0].shape[1], axis=1
+    )
     out_full, kv_full = (
         lax.all_gather(out_weight, "seq", axis=0, tiled=True),
         lax.all_gather(kv_weight, "seq", axis=0, tiled=True),

time: 393 us -> 350 us (0.89)
  waiting for transfers between devices: 280 us -> 211 us
  starting transfers between devices: 0.2 us -> 15.3 us
  local copies, waits for them, and re-layouts: 4.19 us -> 16.4 us
    all_gather x1, waiting for transfers between devices: 64.4 us -> 0.01 us  [on_device(): lax.all_gather(out_weight, 'seq', axis=0, tiled=True)]
    ppermute x0 -> x7, waiting for transfers between devices: none -> 57.8 us  [on_device(): lax.ppermute(ring[-1], 'head', [(dev, (dev + 1) % 8) for dev in range(8)])]
    all_gather x1 -> x0, waiting for transfers between devices: 43.4 us -> none  [on_device(): all_heads = lax.all_gather(mixed, 'head', axis=1, tiled=True)]
    all_gather x1, waiting for transfers between devices: 63.8 us -> 44.5 us  [on_device(): lax.all_gather(kv_weight, 'seq', axis=0, tiled=True)]
    ppermute x0 -> x7, starting transfers between devices: none -> 15.1 us  [on_device(): lax.ppermute(ring[-1], 'head', [(dev, (dev + 1) % 8) for dev in range(8)])]
    unnamed x13 -> x28, local copies, waits for them, and re-layouts: 1.51 us -> 12.9 us
  transfers between devices with their start and end apart: 5 -> 11, of which waited for: 5 -> 10; matrix products, arithmetic and copies ran while one was open for 6% -> 11% of each run, Pallas kernels for 0% -> 0%
where the time goes in v1:
time: 350 us; the launch traced here: 347 us
  waiting for transfers between devices  211 us (60%)
  blocking collectives  59.6 us (17%)
  other arithmetic  19.5 us (6%)
  local copies, waits for them, and re-layouts  16.4 us (5%)
  starting transfers between devices  15.3 us (4%)
  between operations  14 us (4%)
  matrix products  11.3 us (3%)
    all_gather x1, waiting for transfers between devices, entering(): gathered = jax.tree.map(lambda a: lax.all_gather(a, axis), part)  63.1 us
    ppermute x7, waiting for transfers between devices, on_device(): lax.ppermute(ring[-1], 'head', [(dev, (dev + 1) % 8) for dev in range(8)])  57.8 us
    all_gather x1, waiting for transfers between devices, on_device(): normalized = lax.all_gather(local_norm, 'head', axis=1, tiled=True)  44.8 us
    all_gather x1, blocking collectives, entering(): gathered = jax.tree.map(lambda a: lax.all_gather(a, axis), part)  44.7 us
    all_gather x1, waiting for transfers between devices, on_device(): lax.all_gather(kv_weight, 'seq', axis=0, tiled=True)  44.5 us
    add x16, other arithmetic, combine_states(): later[0][:, None, None] * earlier[1] + later[1]  17 us
    ppermute x7, starting transfers between devices, on_device(): lax.ppermute(ring[-1], 'head', [(dev, (dev + 1) % 8) for dev in range(8)])  15.1 us
    psum x1, blocking collectives, on_device(): squares = lax.psum(jnp.sum(wide * wide, axis=1), 'head')  14.8 us
  transfers between devices with their start and end apart: 11, of which 10 were waited for; matrix products, arithmetic and copies ran while one was open for 11% of the time, Pallas kernels for 0%

profile of v1, /device:TPU:2, one launch (start us, length us, event | category | flops | bytes accessed | tf_op | source)
XLA Modules:
  0.0 347.5 jit_solution(66699067743579965)
XLA Ops:
  8.0 1.2 reduce-window.6
  9.8 1.1 copy.73
  10.9 2.0 convolution_add_fusion
  13.8 44.7 %all-gather.1 = f32[64,1,4]{2,1,0:T(1,128)S(1)} all-gather(f32[1,1,4]{2,1,0:T(1,128)S(1)} %bitcast.96), channel_id=1, replica_groups=mesh['seq'=64,'head'=8] {'seq'}, dimensions={0}, use_global_device_ids=true | all-gather | bytes 1040 | tf_op jit(solution)/shard_map/all_gather | solution.py:11
  59.4 63.1 %all-gather.13.cloned.1.call-done = f32[256,128,128]{2,1,0:T(8,128)} async-done(((f32[4,128,128]{2,1,0:T(8,128)}), f32[256,128,128]{2,1,0:T(8,128)}) %all-gather.13.cloned.1.call-update) | async-done | bytes 16777232 | tf_op jit(solution)/shard_map/all_gather | solution.py:11
  122.5 17.8 %while.3 = (s32[]{:T(128)}, f32[4,128,128]{2,1,0:T(8,128)S(1)}, s32[]{:T(128)}, f32[64,4]{1,0:T(8,128)S(1)}, f32[64,4,128,128]{3,2,1,0:T(8,128)}, /*index=5*/s32[]{:T(128)}, s32[]{:T(128)}, s32[]{:T(128)}) while((s32[]{:T(128)}, f32[4,128,128]{2,1,0:T(8,128)S(1)}, s32[]{:T(128)}, f32[64,4]{1,0:T(8,128)S(1)}, f32[64,4,128,128]{3,2,1,0:T(8,128)}, ...), condition=%wide.region_3.4_spmd, body=%wide.region_2.3_spmd.sunk | while | flops 131077 | bytes 786607 | solution.py:19
  122.6 1.1 bitcast_add_fusion.2
  123.7 1.1 bitcast_add_fusion.2
  124.8 1.1 bitcast_add_fusion.2
  125.9 1.1 bitcast_add_fusion.2
  127.0 1.1 bitcast_add_fusion.2
  128.1 1.1 bitcast_add_fusion.2
  129.2 1.1 bitcast_add_fusion.2
  130.4 1.1 bitcast_add_fusion.2
  131.5 1.1 bitcast_add_fusion.2
  132.6 1.1 bitcast_add_fusion.2
  133.7 1.1 bitcast_add_fusion.2
  134.8 1.1 bitcast_add_fusion.2
  135.9 1.1 bitcast_add_fusion.2
  137.0 1.1 bitcast_add_fusion.2
  138.1 1.1 bitcast_add_fusion.2
  139.2 1.1 bitcast_add_fusion.2
  142.0 3.4 collective-permute-start
  145.4 8.6 %collective-permute-done = bf16[256,512]{1,0:T(8,128)(2,1)S(1)} collective-permute-done((bf16[256,512]{1,0:T(8,128)(2,1)S(1)}, bf16[256,512]{1,0:T(8,128)(2,1)S(1)}, u32[]{:S(2)}, u32[]{:S(2)}) %collective-permute-start) | collective-permute-done | bytes 262176 | tf_op jit(solution)/shard_map/ppermute | solution.py:93
  153.9 2.2 collective-permute-start.1
  156.2 9.4 %collective-permute-done.1 = bf16[256,512]{1,0:T(8,128)(2,1)S(1)} collective-permute-done((bf16[256,512]{1,0:T(8,128)(2,1)S(1)}, bf16[256,512]{1,0:T(8,128)(2,1)S(1)}, u32[]{:S(2)}, u32[]{:S(2)}) %collective-permute-start.1) | collective-permute-done | bytes 262176 | tf_op jit(solution)/shard_map/ppermute | solution.py:93
  165.6 1.9 collective-permute-start.2
  167.5 9.0 %collective-permute-done.2 = bf16[256,512]{1,0:T(8,128)(2,1)S(1)} collective-permute-done((bf16[256,512]{1,0:T(8,128)(2,1)S(1)}, bf16[256,512]{1,0:T(8,128)(2,1)S(1)}, u32[]{:S(2)}, u32[]{:S(2)}) %collective-permute-start.2) | collective-permute-done | bytes 262176 | tf_op jit(solution)/shard_map/ppermute | solution.py:93
  176.6 1.9 collective-permute-start.3
  178.5 8.1 %collective-permute-done.3 = bf16[256,512]{1,0:T(8,128)(2,1)S(1)} collective-permute-done((bf16[256,512]{1,0:T(8,128)(2,1)S(1)}, bf16[256,512]{1,0:T(8,128)(2,1)S(1)}, u32[]{:S(2)}, u32[]{:S(2)}) %collective-permute-start.3) | collective-permute-done | bytes 262176 | tf_op jit(solution)/shard_map/ppermute | solution.py:93
  186.6 1.9 collective-permute-start.4
  188.5 7.5 %collective-permute-done.4 = bf16[256,512]{1,0:T(8,128)(2,1)S(1)} collective-permute-done((bf16[256,512]{1,0:T(8,128)(2,1)S(1)}, bf16[256,512]{1,0:T(8,128)(2,1)S(1)}, u32[]{:S(2)}, u32[]{:S(2)}) %collective-permute-start.4) | collective-permute-done | bytes 262176 | tf_op jit(solution)/shard_map/ppermute | solution.py:93
  196.1 1.9 collective-permute-start.5
  198.0 7.5 %collective-permute-done.5 = bf16[256,512]{1,0:T(8,128)(2,1)S(1)} collective-permute-done((bf16[256,512]{1,0:T(8,128)(2,1)S(1)}, bf16[256,512]{1,0:T(8,128)(2,1)S(1)}, u32[]{:S(2)}, u32[]{:S(2)}) %collective-permute-start.5) | collective-permute-done | bytes 262176 | tf_op jit(solution)/shard_map/ppermute | solution.py:93
  205.6 1.9 collective-permute-start.6
  207.5 7.5 %collective-permute-done.6 = bf16[256,512]{1,0:T(8,128)(2,1)S(1)} collective-permute-done((bf16[256,512]{1,0:T(8,128)(2,1)S(1)}, bf16[256,512]{1,0:T(8,128)(2,1)S(1)}, u32[]{:S(2)}, u32[]{:S(2)}) %collective-permute-start.6) | collective-permute-done | bytes 262176 | tf_op jit(solution)/shard_map/ppermute | solution.py:93
  215.0 0.8 constant_dynamic-update-slice_fusion.15
  215.8 0.8 constant_dynamic-update-slice_fusion.14
  216.6 0.8 constant_dynamic-update-slice_fusion.13
  217.4 0.8 constant_dynamic-update-slice_fusion.12
  221.9 0.8 constant_dynamic-update-slice_fusion.6
  225.6 0.8 constant_dynamic-update-slice_fusion.1
  227.2 4.2 %multiply_reduce_fusion = (f32[256]{0:T(256)S(1)}, f32[256,512]{1,0:T(8,128)S(1)}) fusion(bf16[4096,512]{1,0:T(8,128)(2,1)} %all-gather.7.cloned.1.call-done, bf16[256,8192]{1,0:T(8,128)(2,1)} %constant_dynamic-update-slice_fusion, s32[]{:T(128)S(6)} %select_n.34, bf16[256,512]{1,0:T(8,128)(2,1)S(1)} %copy-done.4), kind=kOutput, calls=%fused_computation.24 | convolution fusion | flops 1074528000 | bytes 7078916 | tf_op jit(solution)/shard_map/dot_general | solution.py:101
  231.4 14.8 %psum.7 = f32[256]{0:T(256)S(1)} all-reduce(f32[256]{0:T(256)S(1)} %get-tuple-element.97), channel_id=1, replica_groups=mesh['seq'=64,'head'=8] {'head'}, use_global_device_ids=true, to_apply=%region_6.7 | all-reduce | flops 256 | bytes 2048 | tf_op jit(solution)/shard_map/psum | solution.py:104
  246.2 0.8 multiply_convert_fusion
  247.1 44.5 %all-gather.11.cloned.1.call-done = bf16[4096,256]{1,0:T(8,128)(2,1)} async-done(((bf16[64,256]{1,0:T(8,128)(2,1)}), bf16[4096,256]{1,0:T(8,128)(2,1)}) %all-gather.11.cloned.1.call-update) | async-done | bytes 2097168 | tf_op jit(solution)/shard_map/all_gather | solution.py:99
  291.5 44.8 %all-gather.9.cloned.1.call-done = bf16[256,4096]{1,0:T(8,128)(2,1)} async-done(((bf16[256,512]{1,0:T(8,128)(2,1)}), bf16[256,4096]{1,0:T(8,128)(2,1)}) %all-gather.9.cloned.1.call-update) | async-done | bytes 2097168 | tf_op jit(solution)/shard_map/all_gather | solution.py:108
  336.3 3.1 convolution_convert_fusion
  (71 shorter events, 13.8 us)
Async XLA Ops:
  7.2 51.4 %copy-start = (bf16[256,512]{1,0:T(8,128)(2,1)S(1)}, bf16[256,512]{1,0:T(8,128)(2,1)}, u32[]{:S(2)}) copy-start(bf16[256,512]{1,0:T(8,128)(2,1)} %param.11) | copy-start | bytes 786436
  7.2 115.3 %all-gather.13.cloned.1.call-start = ((), (), s32[]{:S(2)}) async-start(), calls=%async_computation.3 | async-start | bytes 17039360 | tf_op jit(solution)/shard_map/all_gather | solution.py:11
  13.0 214.2 %all-gather.7.cloned.1.call-start = ((), (), s32[]{:S(2)}) async-start(), calls=%async_computation | async-start | bytes 4259840 | tf_op jit(solution)/shard_map/all_gather | solution.py:98
  13.8 277.8 %all-gather.11.cloned.1.call-start = ((), (), s32[]{:S(2)}) async-start(), calls=%async_computation.2 | async-start | bytes 2129920 | tf_op jit(solution)/shard_map/all_gather | solution.py:99
  58.6 82.2 %copy-start.1 = (bf16[256,512]{1,0:T(8,128)(2,1)S(1)}, bf16[256,512]{1,0:T(8,128)(2,1)}, u32[]{:S(2)}) copy-start(bf16[256,512]{1,0:T(8,128)(2,1)} %param.13) | copy-start | bytes 786436
  122.5 19.3 %copy-start.2 = (bf16[256,512]{1,0:T(8,128)(2,1)S(1)}, bf16[256,512]{1,0:T(8,128)(2,1)}, u32[]{:S(2)}) copy-start(bf16[256,512]{1,0:T(8,128)(2,1)} %param.14) | copy-start | bytes 786436
  140.3 67.2 %copy-start.3 = (bf16[512]{0:T(512)(128)(2,1)S(1)}, bf16[512]{0:T(512)(128)(2,1)}, u32[]{:S(2)}) copy-start(bf16[512]{0:T(512)(128)(2,1)} %param.18) | copy-start | bytes 3076
  142.0 12.0 %collective-permute-start = (bf16[256,512]{1,0:T(8,128)(2,1)S(1)}, bf16[256,512]{1,0:T(8,128)(2,1)S(1)}, u32[]{:S(2)}, u32[]{:S(2)}) collective-permute-start(bf16[256,512]{1,0:T(8,128)(2,1)S(1)} %fusion.21), channel_id=1, source_target_pairs={{0,1},{1,2},{2,3},{3,4},{4,5},{5,6},{6,7},{7,0},{8,9},{9,10},{10,1... | collective-permute-start | bytes 786440 | tf_op jit(solution)/shard_map/ppermute | solution.py:93
  153.9 11.7 %collective-permute-start.1 = (bf16[256,512]{1,0:T(8,128)(2,1)S(1)}, bf16[256,512]{1,0:T(8,128)(2,1)S(1)}, u32[]{:S(2)}, u32[]{:S(2)}) collective-permute-start(bf16[256,512]{1,0:T(8,128)(2,1)S(1)} %collective-permute-done), channel_id=1, source_target_pairs={{0,1},{1,2},{2,3},{3,4},{4,5},{5,6},{6,7},{7,0},{8,9},{9,10},{10,1... | collective-permute-start | bytes 786440 | tf_op jit(solution)/shard_map/ppermute | solution.py:93
  156.1 180.2 %all-gather.9.cloned.1.call-start = ((), (), s32[]{:S(2)}) async-start(), calls=%async_computation.1 | async-start | bytes 2359296 | tf_op jit(solution)/shard_map/all_gather | solution.py:108
  165.6 11.0 %collective-permute-start.2 = (bf16[256,512]{1,0:T(8,128)(2,1)S(1)}, bf16[256,512]{1,0:T(8,128)(2,1)S(1)}, u32[]{:S(2)}, u32[]{:S(2)}) collective-permute-start(bf16[256,512]{1,0:T(8,128)(2,1)S(1)} %collective-permute-done.1), channel_id=1, source_target_pairs={{0,1},{1,2},{2,3},{3,4},{4,5},{5,6},{6,7},{7,0},{8,9},{9,10},{10,1... | collective-permute-start | bytes 786440 | tf_op jit(solution)/shard_map/ppermute | solution.py:93
  176.6 10.1 %collective-permute-start.3 = (bf16[256,512]{1,0:T(8,128)(2,1)S(1)}, bf16[256,512]{1,0:T(8,128)(2,1)S(1)}, u32[]{:S(2)}, u32[]{:S(2)}) collective-permute-start(bf16[256,512]{1,0:T(8,128)(2,1)S(1)} %collective-permute-done.2), channel_id=1, source_target_pairs={{0,1},{1,2},{2,3},{3,4},{4,5},{5,6},{6,7},{7,0},{8,9},{9,10},{10,1... | collective-permute-start | bytes 786440 | tf_op jit(solution)/shard_map/ppermute | solution.py:93
  186.6 9.5 %collective-permute-start.4 = (bf16[256,512]{1,0:T(8,128)(2,1)S(1)}, bf16[256,512]{1,0:T(8,128)(2,1)S(1)}, u32[]{:S(2)}, u32[]{:S(2)}) collective-permute-start(bf16[256,512]{1,0:T(8,128)(2,1)S(1)} %collective-permute-done.3), channel_id=1, source_target_pairs={{0,1},{1,2},{2,3},{3,4},{4,5},{5,6},{6,7},{7,0},{8,9},{9,10},{10,1... | collective-permute-start | bytes 786440 | tf_op jit(solution)/shard_map/ppermute | solution.py:93
  196.1 9.5 %collective-permute-start.5 = (bf16[256,512]{1,0:T(8,128)(2,1)S(1)}, bf16[256,512]{1,0:T(8,128)(2,1)S(1)}, u32[]{:S(2)}, u32[]{:S(2)}) collective-permute-start(bf16[256,512]{1,0:T(8,128)(2,1)S(1)} %collective-permute-done.4), channel_id=1, source_target_pairs={{0,1},{1,2},{2,3},{3,4},{4,5},{5,6},{6,7},{7,0},{8,9},{9,10},{10,1... | collective-permute-start | bytes 786440 | tf_op jit(solution)/shard_map/ppermute | solution.py:93
  205.6 9.5 %collective-permute-start.6 = (bf16[256,512]{1,0:T(8,128)(2,1)S(1)}, bf16[256,512]{1,0:T(8,128)(2,1)S(1)}, u32[]{:S(2)}, u32[]{:S(2)}) collective-permute-start(bf16[256,512]{1,0:T(8,128)(2,1)S(1)} %collective-permute-done.5), channel_id=1, source_target_pairs={{0,1},{1,2},{2,3},{3,4},{4,5},{5,6},{6,7},{7,0},{8,9},{9,10},{10,1... | collective-permute-start | bytes 786440 | tf_op jit(solution)/shard_map/ppermute | solution.py:93
  207.5 19.7 %copy-start.4 = (bf16[256,512]{1,0:T(8,128)(2,1)S(1)}, bf16[256,512]{1,0:T(8,128)(2,1)}, u32[]{:S(2)}) copy-start(bf16[256,512]{1,0:T(8,128)(2,1)} %param.15) | copy-start | bytes 786436
Sparse Core Ops, SparseCore 0:
  13.1 109.3 all-gather.12
  125.8 81.7 all-gather.6
  211.0 80.4 all-gather.10
  293.4 42.8 all-gather.8
